TPU v7x, 32 devices: a whole 2x2x4 slice. The times are simulated.
32 devices in a mesh: section: 4 (over x, core), seq: 8 (over z, y).
Axes of the slice: x: 2, y: 2, z: 4, core: 2. Of those that a mesh axis runs over, the one named last changes fastest.
Arguments:
- hidden: bfloat16 [2, 1024, 2688], P(None, 'seq'), may hold values from -6 to 6
- lengths: int32 [2], replicated, may hold values from 512 to 1024, as said below
- reward_pos: int32 [2], replicated, may hold values from 384 to 1023, as said below
- in_gain: bfloat16 [2688], P('seq'), may hold values from 0.099609375 to 1.8984375
- w_query: bfloat16 [2688, 2048], P('seq', 'section'), may hold values from -0.077151675 to 0.077151675
- w_key: bfloat16 [2688, 1024], P('seq', 'section'), may hold values from -0.077151675 to 0.077151675
- w_value: bfloat16 [2688, 1024], P('seq', 'section'), may hold values from -0.125 to 0.125
- query_gain: float32 [128], replicated, may hold values from 0.6 to 7
- key_gain: float32 [128], replicated, may hold values from 0.6 to 7
- w_out: bfloat16 [2048, 2688], P('section', 'seq'), may hold values from -0.125 to 0.125
- post_gain: bfloat16 [2688], P('seq'), may hold values from 0.099609375 to 1.8984375
- final_gain: bfloat16 [2688], P('seq'), may hold values from 0.099609375 to 1.8984375
- value_head: bfloat16 [2688], P('seq'), may hold values from -0.125 to 0.125
Outputs:
- token_values: float32 [2, 1024], P(None, 'seq')
- reward: float32 [2], replicated
Inputs may be any that keep to these rules, and one draw needn't show every extreme that they name: `lengths`: in every draw at least one micro-batch has all 1024 tokens valid. reward_pos[m] lies among the last 128 valid tokens of micro-batch m.
All inputs are finite; a program needn't handle non-finite values.
Results may differ from a plain program's by a relative error of at most 0.01.
Values may be sent and summed in bfloat16 or wider, within the bound.
A program may use at most 64 MiB of HBM per device.

v0:
```python
import jax
import jax.numpy as jnp
from jax import lax
from jax.sharding import PartitionSpec as P

HD = 128
GROUP = 2
WINDOW = 1024
norm_eps = 1e-06
query_scale = 168.0 ** (-0.5)
rope_base = 10000.0


def passed_along(array, axis, by):
    devices = lax.axis_size(axis)
    pairs = [(i, i + by) for i in range(devices) if 0 <= i + by < devices]
    return lax.ppermute(array, axis, pairs)


def rms_scale(values, gain_vec):
    return (
        values * lax.rsqrt(jnp.mean(values * values, axis=-1, keepdims=True) + norm_eps) * gain_vec
    )


def rotate_pairs(head_rows, positions):
    half_width = head_rows.shape[-1] // 2
    frequency = rope_base ** (
        -jnp.arange(half_width, dtype=jnp.float32) * 2.0 / head_rows.shape[-1]
    )
    angles = positions.astype(jnp.float32)[:, None] * frequency[None, :]
    target = (angles.shape[0],) + (1,) * (head_rows.ndim - 2) + (half_width,)
    cosine = jnp.cos(angles).reshape(target)
    sine_part = jnp.sin(angles).reshape(target)
    front_half = head_rows[..., :half_width]
    back_half = head_rows[..., half_width:]
    return jnp.concatenate(
        [front_half * cosine - back_half * sine_part, back_half * cosine + front_half * sine_part],
        axis=-1,
    )


def window_blocks(packed, tok_dev):
    block_count = WINDOW // tok_dev + 1
    blocks_held = [packed]
    for offset in range(1, block_count):
        blocks_held.append(passed_along(packed, "seq", offset))
    return jnp.concatenate(blocks_held[::-1], axis=1)


def window_attention(queries, keys_all, values_all, query_pos, key_pos):
    scores = jnp.einsum("qhgd,khd->hgqk", queries, keys_all, preferred_element_type=jnp.float32)
    allowed = (
        (key_pos[None, :] <= query_pos[:, None])
        & (key_pos[None, :] > query_pos[:, None] - WINDOW)
        & (key_pos[None, :] >= 0)
    )
    scores = jnp.where(allowed[None, None], scores, -1e30)
    row_top = jnp.max(scores, axis=-1, keepdims=True)
    exponent = jnp.exp(scores - row_top)
    attn_weights = (exponent / jnp.sum(exponent, axis=-1, keepdims=True)).astype(jnp.bfloat16)
    mixed_heads = jnp.einsum(
        "hgqk,khd->qhgd", attn_weights, values_all, preferred_element_type=jnp.float32
    )
    return mixed_heads.astype(jnp.bfloat16)


def local(
    hidden,
    lengths,
    reward_pos,
    in_gain,
    w_query,
    w_key,
    w_value,
    query_gain,
    key_gain,
    w_out,
    post_gain,
    final_gain,
    value_head,
):
    micro_count, tok_dev, width = hidden.shape
    row_count = micro_count * tok_dev
    qwidth = w_query.shape[1]
    kwidth = w_key.shape[1]
    heads_here = kwidth // HD
    widened = hidden.reshape(row_count, width).astype(jnp.float32)
    inverse = lax.rsqrt(jnp.mean(widened * widened, axis=-1, keepdims=True) + norm_eps)
    seq_pos = lax.axis_index("seq") * tok_dev + jnp.arange(tok_dev, dtype=jnp.int32)
    positions = jnp.tile(seq_pos, micro_count)
    gain_piece = lax.all_gather(in_gain, "seq", axis=0, tiled=True)
    query_piece = lax.all_gather(w_query, "seq", axis=0, tiled=True)
    key_piece = lax.all_gather(w_key, "seq", axis=0, tiled=True)
    value_piece = lax.all_gather(w_value, "seq", axis=0, tiled=True)
    post_piece = lax.all_gather(post_gain, "seq", axis=0, tiled=True)
    final_piece = lax.all_gather(final_gain, "seq", axis=0, tiled=True)
    head_piece = lax.all_gather(value_head, "seq", axis=0, tiled=True)
    normed = (widened * inverse * gain_piece.astype(jnp.float32)).astype(jnp.bfloat16)
    query_acc = jnp.dot(normed, query_piece, preferred_element_type=jnp.float32)
    key_acc = jnp.dot(normed, key_piece, preferred_element_type=jnp.float32)
    value_acc = jnp.dot(normed, value_piece, preferred_element_type=jnp.float32)
    post_full = post_piece.astype(jnp.float32)
    final_full = final_piece.astype(jnp.float32)
    head_full = head_piece.astype(jnp.float32)
    folded = (query_acc, key_acc, value_acc, post_full, final_full, head_full)
    queries = folded[0].reshape(row_count, heads_here, GROUP, HD)
    queries = (rotate_pairs(rms_scale(queries, query_gain), positions) * query_scale).astype(
        jnp.bfloat16
    )
    keys_new = folded[1].reshape(row_count, heads_here, HD)
    keys_new = (
        rotate_pairs(rms_scale(keys_new, key_gain), positions)
        .astype(jnp.bfloat16)
        .reshape(row_count, kwidth)
    )
    vals_new = folded[2].astype(jnp.bfloat16)
    packed = jnp.concatenate([keys_new, vals_new], axis=1).reshape(micro_count, tok_dev, 2 * kwidth)
    window_rows = window_blocks(packed, tok_dev)
    key_pos = seq_pos[0] - WINDOW + jnp.arange(WINDOW + tok_dev, dtype=jnp.int32)
    mixed_list = []
    for micro_id in range(micro_count):
        block_queries = queries[micro_id * tok_dev : (micro_id + 1) * tok_dev]
        keys_all = window_rows[micro_id, :, :kwidth].reshape(-1, heads_here, HD)
        values_all = window_rows[micro_id, :, kwidth:].reshape(-1, heads_here, HD)
        mixed_list.append(
            window_attention(block_queries, keys_all, values_all, seq_pos, key_pos).reshape(
                tok_dev, qwidth
            )
        )
    mixed_all = jnp.concatenate(mixed_list, axis=0)
    branch = jnp.dot(
        mixed_all,
        lax.all_gather(w_out, "seq", axis=1, tiled=True),
        preferred_element_type=jnp.float32,
    )
    post_full, final_full, head_full = (folded[3], folded[4], folded[5])
    share_width = width // lax.axis_size("section")
    offset = lax.axis_index("section") * share_width
    share = lax.psum_scatter(branch, "section", scatter_dimension=1, tiled=True)
    branch_sq = lax.psum(jnp.sum(share * share, axis=1), "section")
    share_scale = lax.rsqrt(branch_sq / width + norm_eps)[:, None]
    post_share = lax.dynamic_slice_in_dim(post_full, offset, share_width, 0)
    updated = (
        lax.dynamic_slice_in_dim(widened, offset, share_width, 1) + share * share_scale * post_share
    ).astype(jnp.bfloat16)
    updated_wide = updated.astype(jnp.float32)
    residual_sq = lax.psum(jnp.sum(updated_wide * updated_wide, axis=1), "section")
    final_share = lax.dynamic_slice_in_dim(final_full, offset, share_width, 0)
    last_rows = (
        updated_wide * lax.rsqrt(residual_sq / width + norm_eps)[:, None] * final_share
    ).astype(jnp.bfloat16)
    head_share = lax.dynamic_slice_in_dim(head_full, offset, share_width, 0).astype(jnp.bfloat16)
    raw_values = lax.psum(
        jnp.dot(last_rows, head_share, preferred_element_type=jnp.float32), "section"
    )
    raw_values = raw_values.reshape(micro_count, tok_dev)
    token_values = jnp.where(seq_pos[None, :] < lengths[:, None], raw_values, 0.0)
    partial_value = jnp.sum(
        jnp.where(seq_pos[None, :] == reward_pos[:, None], token_values, 0.0), axis=1
    )
    reward = lax.psum(partial_value, "seq")
    return (token_values, reward)


def solution(mesh):
    placed = (
        P(None, "seq", None),
        P(),
        P(),
        P("seq"),
        P("seq", "section"),
        P("seq", "section"),
        P("seq", "section"),
        P(),
        P(),
        P("section", "seq"),
        P("seq"),
        P("seq"),
        P("seq"),
    )
    return jax.shard_map(
        local, mesh=mesh, in_specs=placed, out_specs=(P(None, "seq"), P()), check_vma=False
    )
```

profile of v0, /device:TPU:0, one launch (start us, length us, event | category | flops | bytes accessed | tf_op | source)
XLA Modules:
  0.0 331.5 jit_solution(10913897586998984354)
XLA Ops:
  15.5 39.5 %all-reduce.4 = (bf16[2688]{0:T(1024)(128)(2,1)S(1)}, bf16[2688]{0:T(1024)(128)(2,1)S(1)}, bf16[2688]{0:T(1024)(128)(2,1)S(1)}, bf16[2688]{0:T(1024)(128)(2,1)S(1)}) all-reduce(bf16[2688]{0:T(1024)(128)(2,1)S(1)} %dynamic-update-slice.3, bf16[2688]{0:T(1024)(128)(2,1)S(1)} %dynamic-update-slice, ...), channel_id=1, replica_groups=mesh['section'=4,'seq'=8] {'seq'}, use_global_device_ids=true, to_apply=%add.3 | all-reduce | flops 10752 | bytes 43008
  55.1 1.7 multiply_reduce_fusion
  56.8 1.7 copy.43
  58.4 2.9 multiply_convert_fusion.1
  61.7 2.6 copy.24
  64.3 2.4 multiply_reduce_fusion.3
  66.9 31.5 %all-gather.7.cloned.1.call-done = bf16[2688,256]{1,0:T(8,128)(2,1)} async-done(((bf16[336,256]{1,0:T(8,128)(2,1)}), bf16[2688,256]{1,0:T(8,128)(2,1)}) %all-gather.7.cloned.1.call-update) | async-done | bytes 1376272 | tf_op jit(solution)/shard_map/all_gather | solution.py:95
  98.4 2.4 fusion.15
  101.6 4.0 %collective-permute-start.1 = (bf16[2,128,512]{1,2,0:T(8,128)(2,1)S(1)}, bf16[2,128,512]{1,2,0:T(8,128)(2,1)S(1)}, u32[]{:S(2)}, u32[]{:S(2)}) collective-permute-start(bf16[2,128,512]{1,2,0:T(8,128)(2,1)S(1)} %pad_maximum_fusion), channel_id=1, source_target_pairs={{0,7},{8,15},{16,23},{24,31}} | collective-permute-start | bytes 786440 | tf_op jit(solution)/shard_map/ppermute | solution.py:17
  106.9 1.5 and_and_fusion
  111.0 2.4 collective-permute-start.5
  113.6 2.9 collective-permute-done.1
  117.8 9.9 %collective-permute-done.2 = bf16[2,128,512]{1,2,0:T(8,128)(2,1)S(1)} collective-permute-done((bf16[2,128,512]{1,2,0:T(8,128)(2,1)S(1)}, bf16[2,128,512]{1,2,0:T(8,128)(2,1)S(1)}, u32[]{:S(2)}, u32[]{:S(2)}) %collective-permute-start.2) | collective-permute-done | bytes 262176 | tf_op jit(solution)/shard_map/ppermute | solution.py:17
  127.7 1.5 collective-permute-start.7
  129.2 5.3 %collective-permute-done.3 = bf16[2,128,512]{1,2,0:T(8,128)(2,1)S(1)} collective-permute-done((bf16[2,128,512]{1,2,0:T(8,128)(2,1)S(1)}, bf16[2,128,512]{1,2,0:T(8,128)(2,1)S(1)}, u32[]{:S(2)}, u32[]{:S(2)}) %collective-permute-start.3) | collective-permute-done | bytes 262176 | tf_op jit(solution)/shard_map/ppermute | solution.py:17
  134.6 5.6 %collective-permute-done.4 = bf16[2,128,512]{1,2,0:T(8,128)(2,1)S(1)} collective-permute-done((bf16[2,128,512]{1,2,0:T(8,128)(2,1)S(1)}, bf16[2,128,512]{1,2,0:T(8,128)(2,1)S(1)}, u32[]{:S(2)}, u32[]{:S(2)}) %collective-permute-start.4) | collective-permute-done | bytes 262176 | tf_op jit(solution)/shard_map/ppermute | solution.py:17
  140.3 5.6 %collective-permute-done.5 = bf16[2,128,512]{1,2,0:T(8,128)(2,1)S(1)} collective-permute-done((bf16[2,128,512]{1,2,0:T(8,128)(2,1)S(1)}, bf16[2,128,512]{1,2,0:T(8,128)(2,1)S(1)}, u32[]{:S(2)}, u32[]{:S(2)}) %collective-permute-start.5) | collective-permute-done | bytes 262176 | tf_op jit(solution)/shard_map/ppermute | solution.py:17
  145.9 3.4 %collective-permute-done.6 = bf16[2,128,512]{1,2,0:T(8,128)(2,1)S(1)} collective-permute-done((bf16[2,128,512]{1,2,0:T(8,128)(2,1)S(1)}, bf16[2,128,512]{1,2,0:T(8,128)(2,1)S(1)}, u32[]{:S(2)}, u32[]{:S(2)}) %collective-permute-start.6) | collective-permute-done | bytes 262176 | tf_op jit(solution)/shard_map/ppermute | solution.py:17
  150.8 27.7 %all-gather.9.cloned.1.call-done = bf16[2688,512]{1,0:T(8,128)(2,1)} async-done(((bf16[336,512]{1,0:T(8,128)(2,1)}), bf16[2688,512]{1,0:T(8,128)(2,1)}) %all-gather.9.cloned.1.call-update) | async-done | bytes 2752528 | tf_op jit(solution)/shard_map/all_gather | solution.py:93
  178.5 4.5 %copy.27 = bf16[512,2688]{1,0:T(8,128)(2,1)} copy(bf16[512,2688]{0,1:T(8,128)(2,1)} %bitcast.94) | data formatting | bytes 5505024 | tf_op jit(solution)/shard_map/dot_general | solution.py:100
  183.0 3.2 multiply_reduce_fusion.2
  187.1 2.1 fusion.64
  189.2 1.8 fusion.61
  191.1 3.2 fusion.14
  194.3 3.1 fusion.13
  197.3 46.1 %all-gather.11.cloned.1.call-done = bf16[512,2688]{0,1:T(8,128)(2,1)} async-done(((bf16[512,336]{0,1:T(8,128)(2,1)}), bf16[512,2688]{0,1:T(8,128)(2,1)}) %all-gather.11.cloned.1.call-update) | async-done | bytes 2752528 | tf_op jit(solution)/shard_map/all_gather | solution.py:134
  243.4 4.3 %fusion.24 = f32[256,2688]{0,1:T(8,128)} fusion(bf16[512,2688]{0,1:T(8,128)(2,1)} %all-gather.11.cloned.1.call-done, bf16[128,512]{0,1:T(8,128)(2,1)} %bitcast.108, bf16[128,512]{0,1:T(8,128)(2,1)} %bitcast.107), kind=kOutput, calls=%fused_computation.39 | convolution fusion | flops 705167360 | bytes 5767168 | tf_op jit(solution)/shard_map/dot_general | solution.py:132
  248.0 33.8 %reduce-scatter.2.cloned.1.call-done = f32[256,672]{0,1:T(8,128)} async-done(((f32[256,2688]{0,1:T(8,128)}), f32[256,672]{0,1:T(8,128)}) %reduce-scatter.2.cloned.1.call-update) | async-done | bytes 688144 | tf_op jit(solution)/shard_map/reduce_scatter | solution.py:140
  283.0 5.8 %psum.28 = f32[256]{0:T(256)S(1)} all-reduce(f32[256]{0:T(256)S(1)} %multiply_reduce_fusion.1), channel_id=1, replica_groups=mesh['section'=4,'seq'=8] {'section'}, use_global_device_ids=true, to_apply=%region_9.10 | all-reduce | flops 256 | bytes 2048 | tf_op jit(solution)/shard_map/psum | solution.py:141
  290.1 5.7 %psum.29 = f32[256]{0:T(256)S(1)} all-reduce(f32[256]{0:T(256)S(1)} %get-tuple-element.8), channel_id=1, replica_groups=mesh['section'=4,'seq'=8] {'section'}, use_global_device_ids=true, to_apply=%region_11.12 | all-reduce | flops 256 | bytes 2048 | tf_op jit(solution)/shard_map/psum | solution.py:148
  296.0 6.3 %psum.30 = f32[2,128]{1,0:T(2,128)S(1)} all-reduce(f32[2,128]{1,0:T(2,128)S(1)} %bitcast.110), channel_id=1, replica_groups=mesh['section'=4,'seq'=8] {'section'}, use_global_device_ids=true, to_apply=%region_12.13 | all-reduce | flops 256 | bytes 2048 | tf_op jit(solution)/shard_map/psum | solution.py:154
  303.1 21.9 %psum.31 = f32[2]{0:T(128)} all-reduce(f32[2]{0:T(128)S(1)} %get-tuple-element.6), channel_id=1, replica_groups=mesh['section'=4,'seq'=8] {'seq'}, use_global_device_ids=true, to_apply=%region_14.15 | all-reduce | flops 2 | bytes 16 | tf_op jit(solution)/shard_map/psum | solution.py:162
  (78 shorter events, 20.7 us)
Async XLA Ops:
  7.2 54.5 %all-gather.5.cloned.1.call-start = ((), (), s32[]{:S(2)}) async-start(), calls=%async_computation.1 | async-start | bytes 1548288 | tf_op jit(solution)/shard_map/all_gather | solution.py:94
  7.9 90.5 %all-gather.7.cloned.1.call-start = ((), (), s32[]{:S(2)}) async-start(), calls=%async_computation.2 | async-start | bytes 1548288 | tf_op jit(solution)/shard_map/all_gather | solution.py:95
  8.6 169.8 %all-gather.9.cloned.1.call-start = ((), (), s32[]{:S(2)}) async-start(), calls=%async_computation.3 | async-start | bytes 3096576 | tf_op jit(solution)/shard_map/all_gather | solution.py:93
  9.4 234.0 %all-gather.11.cloned.1.call-start = ((), (), s32[]{:S(2)}) async-start(), calls=%async_computation.4 | async-start | bytes 3096576 | tf_op jit(solution)/shard_map/all_gather | solution.py:134
  10.0 271.8 %reduce-scatter.2.cloned.1.call-start = ((), (), s32[]{:S(2)}) async-start(), calls=%async_computation.5 | async-start | bytes 3440640 | tf_op jit(solution)/shard_map/reduce_scatter | solution.py:140
  61.7 5.0 %copy-start.1 = (f32[128]{0:T(128)S(1)}, f32[128]{0:T(128)}, u32[]{:S(2)}) copy-start(f32[128]{0:T(128)} %param.21) | copy-start | bytes 1540
  100.9 10.1 %collective-permute-start = (bf16[2,128,512]{1,2,0:T(8,128)(2,1)S(1)}, bf16[2,128,512]{1,2,0:T(8,128)(2,1)S(1)}, u32[]{:S(2)}, u32[]{:S(2)}) collective-permute-start(bf16[2,128,512]{1,2,0:T(8,128)(2,1)S(1)} %pad_maximum_fusion), channel_id=1, source_target_pairs={} | collective-permute-start | bytes 786440 | tf_op jit(solution)/shard_map/ppermute | solution.py:17
  101.6 14.9 %collective-permute-start.1 = (bf16[2,128,512]{1,2,0:T(8,128)(2,1)S(1)}, bf16[2,128,512]{1,2,0:T(8,128)(2,1)S(1)}, u32[]{:S(2)}, u32[]{:S(2)}) collective-permute-start(bf16[2,128,512]{1,2,0:T(8,128)(2,1)S(1)} %pad_maximum_fusion), channel_id=1, source_target_pairs={{0,7},{8,15},{16,23},{24,31}} | collective-permute-start | bytes 786440 | tf_op jit(solution)/shard_map/ppermute | solution.py:17
  105.6 22.1 %collective-permute-start.2 = (bf16[2,128,512]{1,2,0:T(8,128)(2,1)S(1)}, bf16[2,128,512]{1,2,0:T(8,128)(2,1)S(1)}, u32[]{:S(2)}, u32[]{:S(2)}) collective-permute-start(bf16[2,128,512]{1,2,0:T(8,128)(2,1)S(1)} %pad_maximum_fusion), channel_id=1, source_target_pairs={{0,6},{1,7},{8,14},{9,15},{16,22},{17,23},{24,30},{25,31}} | collective-permute-start | bytes 786440 | tf_op jit(solution)/shard_map/ppermute | solution.py:17
  108.4 26.2 %collective-permute-start.3 = (bf16[2,128,512]{1,2,0:T(8,128)(2,1)S(1)}, bf16[2,128,512]{1,2,0:T(8,128)(2,1)S(1)}, u32[]{:S(2)}, u32[]{:S(2)}) collective-permute-start(bf16[2,128,512]{1,2,0:T(8,128)(2,1)S(1)} %pad_maximum_fusion), channel_id=1, source_target_pairs={{0,5},{1,6},{2,7},{8,13},{9,14},{10,15},{16,21},{17,22},{18,23},{2... | collective-permute-start | bytes 786440 | tf_op jit(solution)/shard_map/ppermute | solution.py:17
  109.7 30.5 %collective-permute-start.4 = (bf16[2,128,512]{1,2,0:T(8,128)(2,1)S(1)}, bf16[2,128,512]{1,2,0:T(8,128)(2,1)S(1)}, u32[]{:S(2)}, u32[]{:S(2)}) collective-permute-start(bf16[2,128,512]{1,2,0:T(8,128)(2,1)S(1)} %pad_maximum_fusion), channel_id=1, source_target_pairs={{0,4},{1,5},{2,6},{3,7},{8,12},{9,13},{10,14},{11,15},{16,20},{17,... | collective-permute-start | bytes 786440 | tf_op jit(solution)/shard_map/ppermute | solution.py:17
  111.0 34.8 %collective-permute-start.5 = (bf16[2,128,512]{1,2,0:T(8,128)(2,1)S(1)}, bf16[2,128,512]{1,2,0:T(8,128)(2,1)S(1)}, u32[]{:S(2)}, u32[]{:S(2)}) collective-permute-start(bf16[2,128,512]{1,2,0:T(8,128)(2,1)S(1)} %pad_maximum_fusion), channel_id=1, source_target_pairs={{0,3},{1,4},{2,5},{3,6},{4,7},{8,11},{9,12},{10,13},{11,14},{12,15... | collective-permute-start | bytes 786440 | tf_op jit(solution)/shard_map/ppermute | solution.py:17
  116.5 32.9 %collective-permute-start.6 = (bf16[2,128,512]{1,2,0:T(8,128)(2,1)S(1)}, bf16[2,128,512]{1,2,0:T(8,128)(2,1)S(1)}, u32[]{:S(2)}, u32[]{:S(2)}) collective-permute-start(bf16[2,128,512]{1,2,0:T(8,128)(2,1)S(1)} %pad_maximum_fusion), channel_id=1, source_target_pairs={{0,2},{1,3},{2,4},{3,5},{4,6},{5,7},{8,10},{9,11},{10,12},{11,13},... | collective-permute-start | bytes 786440 | tf_op jit(solution)/shard_map/ppermute | solution.py:17
  127.7 21.7 %collective-permute-start.7 = (bf16[2,128,512]{1,2,0:T(8,128)(2,1)S(1)}, bf16[2,128,512]{1,2,0:T(8,128)(2,1)S(1)}, u32[]{:S(2)}, u32[]{:S(2)}) collective-permute-start(bf16[2,128,512]{1,2,0:T(8,128)(2,1)S(1)} %pad_maximum_fusion), channel_id=1, source_target_pairs={{0,1},{1,2},{2,3},{3,4},{4,5},{5,6},{6,7},{8,9},{9,10},{10,11},{11... | collective-permute-start | bytes 786440 | tf_op jit(solution)/shard_map/ppermute | solution.py:17
  183.0 3.2 copy-start.2
  186.4 2.9 copy-start
  247.7 54.6 %copy-start.3 = (s32[2]{0:T(128)S(1)}, s32[2]{0:T(128)}, u32[]{:S(2)}) copy-start(s32[2]{0:T(128)} %param.15) | copy-start | bytes 28
  247.7 54.6 %copy-start.4 = (s32[2]{0:T(128)S(1)}, s32[2]{0:T(128)}, u32[]{:S(2)}) copy-start(s32[2]{0:T(128)} %param.14) | copy-start | bytes 28
Sparse Core Ops, SparseCore 0:
  10.2 45.0 all-gather.4
  57.4 40.9 all-gather.6
  100.6 77.8 all-gather.8
  180.5 62.8 all-gather.10
  247.9 33.8 reduce-scatter.1
where the time goes:
time: 332 us; the launch traced here: 331 us
  waiting for transfers between devices  174 us (52%)
  blocking collectives  79.1 us (24%)
  matrix products  22.7 us (7%)
  local copies, waits for them, and re-layouts  15.4 us (5%)
  between operations  14.8 us (4%)
  starting transfers between devices  14 us (4%)
  other arithmetic  11.1 us (3%)
    all_gather x1, waiting for transfers between devices, local(): lax.all_gather(w_out, 'seq', axis=1, tiled=True)  46.1 us
    unnamed x1, blocking collectives  39.5 us
    reduce_scatter x1, waiting for transfers between devices, local(): share = lax.psum_scatter(branch, 'section', scatter_dimension=1, tiled=True)  33.8 us
    ppermute x8, waiting for transfers between devices, passed_along(): return lax.ppermute(array, axis, pairs)  32.7 us
    all_gather x1, waiting for transfers between devices, local(): value_piece = lax.all_gather(w_value, 'seq', axis=0, tiled=True)  31.5 us
    all_gather x1, waiting for transfers between devices, local(): query_piece = lax.all_gather(w_query, 'seq', axis=0, tiled=True)  27.7 us
    psum x1, blocking collectives, local(): reward = lax.psum(partial_value, 'seq')  21.9 us
    ppermute x8, starting transfers between devices, passed_along(): return lax.ppermute(array, axis, pairs)  13.8 us
  transfers between devices with their start and end apart: 13, of which 10 were waited for; matrix products, arithmetic and copies ran while one was open for 12% of the time, Pallas kernels for 0%

commit v1 on v0

--- a/solution.py
+++ b/solution.py
@@ -131,7 +131,7 @@
     mixed_all = jnp.concatenate(mixed_list, axis=0)
     branch = jnp.dot(
         mixed_all,
-        lax.all_gather(w_out, "seq", axis=1, tiled=True),
+        jnp.concatenate(lax.all_gather(w_out, "seq"), axis=1),
         preferred_element_type=jnp.float32,
     )
     post_full, final_full, head_full = (folded[3], folded[4], folded[5])

time: 332 us -> 343 us (1.033)
  waiting for transfers between devices: 174 us -> 185 us
  matrix products: 22.7 us -> 18.2 us
  local copies, waits for them, and re-layouts: 15.4 us -> 18.9 us
    all_gather x1, waiting for transfers between devices: 46.1 us -> 58.2 us  [local(): lax.all_gather(w_out, 'seq')]
    unnamed x27 -> x34, local copies, waits for them, and re-layouts: 5.26 us -> 9.06 us
  transfers between devices with their start and end apart: 13 -> 13, of which waited for: 10 -> 10; matrix products, arithmetic and copies ran while one was open for 12% -> 9% of each run, Pallas kernels for 0% -> 0%
where the time goes in v1:
time: 343 us; the launch traced here: 342 us
  waiting for transfers between devices  185 us (54%)
  blocking collectives  79.1 us (23%)
  local copies, waits for them, and re-layouts  18.9 us (6%)
  matrix products  18.2 us (5%)
  between operations  14.9 us (4%)
  starting transfers between devices  14 us (4%)
  other arithmetic  11.6 us (3%)
    all_gather x1, waiting for transfers between devices, local(): lax.all_gather(w_out, 'seq')  58.2 us
    unnamed x1, blocking collectives  39.5 us
    reduce_scatter x1, waiting for transfers between devices, local(): share = lax.psum_scatter(branch, 'section', scatter_dimension=1, tiled=True)  33.4 us
    ppermute x8, waiting for transfers between devices, passed_along(): return lax.ppermute(array, axis, pairs)  32.7 us
    all_gather x1, waiting for transfers between devices, local(): value_piece = lax.all_gather(w_value, 'seq', axis=0, tiled=True)  30.5 us
    all_gather x1, waiting for transfers between devices, local(): query_piece = lax.all_gather(w_query, 'seq', axis=0, tiled=True)  27.7 us
    psum x1, blocking collectives, local(): reward = lax.psum(partial_value, 'seq')  21.9 us
    ppermute x8, starting transfers between devices, passed_along(): return lax.ppermute(array, axis, pairs)  13.8 us
  transfers between devices with their start and end apart: 13, of which 10 were waited for; matrix products, arithmetic and copies ran while one was open for 9% of the time, Pallas kernels for 0%

profile of v1, /device:TPU:0, one launch (start us, length us, event | category | flops | bytes accessed | tf_op | source)
XLA Modules:
  0.0 341.8 jit_solution(16684824448332908040)
XLA Ops:
  15.5 39.5 %all-reduce.4 = (bf16[2688]{0:T(1024)(128)(2,1)S(1)}, bf16[2688]{0:T(1024)(128)(2,1)S(1)}, bf16[2688]{0:T(1024)(128)(2,1)S(1)}, bf16[2688]{0:T(1024)(128)(2,1)S(1)}) all-reduce(bf16[2688]{0:T(1024)(128)(2,1)S(1)} %dynamic-update-slice.3, bf16[2688]{0:T(1024)(128)(2,1)S(1)} %dynamic-update-slice, ...), channel_id=1, replica_groups=mesh['section'=4,'seq'=8] {'seq'}, use_global_device_ids=true, to_apply=%add.3 | all-reduce | flops 10752 | bytes 43008
  55.1 1.7 multiply_reduce_fusion
  56.8 1.7 copy.55
  58.4 3.9 %multiply_convert_fusion.1 = bf16[2,128,2688]{2,1,0:T(8,128)(2,1)} fusion(bf16[2,128,2688]{2,1,0:T(8,128)(2,1)} %param.13, f32[2688]{0:T(1024)S(1)} %convert_element_type.89, f32[2,128]{1,0:T(2,128)S(1)} %get-tuple-element.20), kind=kLoop, calls=%fused_computation.11 | loop fusion | flops 2752512 | bytes 2764288 | tf_op jit(solution)/shard_map/convert_element_type | solution.py:99
  62.7 2.6 copy.35
  65.3 2.3 multiply_reduce_fusion.3
  67.9 30.5 %all-gather.8.cloned.1.call-done = bf16[2688,256]{1,0:T(8,128)(2,1)} async-done(((bf16[336,256]{1,0:T(8,128)(2,1)}), bf16[2688,256]{1,0:T(8,128)(2,1)}) %all-gather.8.cloned.1.call-update) | async-done | bytes 1376272 | tf_op jit(solution)/shard_map/all_gather | solution.py:95
  98.4 2.4 fusion.15
  101.6 4.0 %collective-permute-start.1 = (bf16[2,128,512]{1,2,0:T(8,128)(2,1)S(1)}, bf16[2,128,512]{1,2,0:T(8,128)(2,1)S(1)}, u32[]{:S(2)}, u32[]{:S(2)}) collective-permute-start(bf16[2,128,512]{1,2,0:T(8,128)(2,1)S(1)} %pad_maximum_fusion), channel_id=1, source_target_pairs={{0,7},{8,15},{16,23},{24,31}} | collective-permute-start | bytes 786440 | tf_op jit(solution)/shard_map/ppermute | solution.py:17
  106.9 1.5 and_and_fusion
  111.1 2.4 collective-permute-start.5
  113.6 2.9 collective-permute-done.1
  117.8 9.9 %collective-permute-done.2 = bf16[2,128,512]{1,2,0:T(8,128)(2,1)S(1)} collective-permute-done((bf16[2,128,512]{1,2,0:T(8,128)(2,1)S(1)}, bf16[2,128,512]{1,2,0:T(8,128)(2,1)S(1)}, u32[]{:S(2)}, u32[]{:S(2)}) %collective-permute-start.2) | collective-permute-done | bytes 262176 | tf_op jit(solution)/shard_map/ppermute | solution.py:17
  127.7 1.5 collective-permute-start.7
  129.3 5.3 %collective-permute-done.3 = bf16[2,128,512]{1,2,0:T(8,128)(2,1)S(1)} collective-permute-done((bf16[2,128,512]{1,2,0:T(8,128)(2,1)S(1)}, bf16[2,128,512]{1,2,0:T(8,128)(2,1)S(1)}, u32[]{:S(2)}, u32[]{:S(2)}) %collective-permute-start.3) | collective-permute-done | bytes 262176 | tf_op jit(solution)/shard_map/ppermute | solution.py:17
  134.7 5.6 %collective-permute-done.4 = bf16[2,128,512]{1,2,0:T(8,128)(2,1)S(1)} collective-permute-done((bf16[2,128,512]{1,2,0:T(8,128)(2,1)S(1)}, bf16[2,128,512]{1,2,0:T(8,128)(2,1)S(1)}, u32[]{:S(2)}, u32[]{:S(2)}) %collective-permute-start.4) | collective-permute-done | bytes 262176 | tf_op jit(solution)/shard_map/ppermute | solution.py:17
  140.3 5.6 %collective-permute-done.5 = bf16[2,128,512]{1,2,0:T(8,128)(2,1)S(1)} collective-permute-done((bf16[2,128,512]{1,2,0:T(8,128)(2,1)S(1)}, bf16[2,128,512]{1,2,0:T(8,128)(2,1)S(1)}, u32[]{:S(2)}, u32[]{:S(2)}) %collective-permute-start.5) | collective-permute-done | bytes 262176 | tf_op jit(solution)/shard_map/ppermute | solution.py:17
  145.9 3.4 %collective-permute-done.6 = bf16[2,128,512]{1,2,0:T(8,128)(2,1)S(1)} collective-permute-done((bf16[2,128,512]{1,2,0:T(8,128)(2,1)S(1)}, bf16[2,128,512]{1,2,0:T(8,128)(2,1)S(1)}, u32[]{:S(2)}, u32[]{:S(2)}) %collective-permute-start.6) | collective-permute-done | bytes 262176 | tf_op jit(solution)/shard_map/ppermute | solution.py:17
  150.8 27.7 %all-gather.10.cloned.1.call-done = bf16[2688,512]{1,0:T(8,128)(2,1)} async-done(((bf16[336,512]{1,0:T(8,128)(2,1)}), bf16[2688,512]{1,0:T(8,128)(2,1)}) %all-gather.10.cloned.1.call-update) | async-done | bytes 2752528 | tf_op jit(solution)/shard_map/all_gather | solution.py:93
  178.5 3.3 copy.38
  181.8 2.3 multiply_reduce_fusion.2
  187.0 58.2 %all-gather.12.cloned.1.call-done = bf16[4096,336]{0,1:T(8,128)(2,1)} async-done(((bf16[512,336]{0,1:T(8,128)(2,1)}), bf16[4096,336]{0,1:T(8,128)(2,1)}) %all-gather.12.cloned.1.call-update) | async-done | bytes 2752528 | tf_op jit(solution)/shard_map/all_gather | solution.py:134
  245.2 3.0 copy.60
  249.2 2.6 fusion.14
  251.7 3.1 fusion.13
  254.8 3.3 fusion.24
  258.5 33.4 %reduce-scatter.2.cloned.1.call-done = f32[256,672]{0,1:T(8,128)} async-done(((f32[256,2688]{0,1:T(8,128)}), f32[256,672]{0,1:T(8,128)}) %reduce-scatter.2.cloned.1.call-update) | async-done | bytes 688144 | tf_op jit(solution)/shard_map/reduce_scatter | solution.py:140
  293.1 5.8 %psum.28 = f32[256]{0:T(256)S(1)} all-reduce(f32[256]{0:T(256)S(1)} %multiply_reduce_fusion.1), channel_id=1, replica_groups=mesh['section'=4,'seq'=8] {'section'}, use_global_device_ids=true, to_apply=%region_9.10 | all-reduce | flops 256 | bytes 2048 | tf_op jit(solution)/shard_map/psum | solution.py:141
  298.9 1.5 fusion.16
  300.4 5.7 %psum.29 = f32[256]{0:T(256)S(1)} all-reduce(f32[256]{0:T(256)S(1)} %get-tuple-element.8), channel_id=1, replica_groups=mesh['section'=4,'seq'=8] {'section'}, use_global_device_ids=true, to_apply=%region_11.12 | all-reduce | flops 256 | bytes 2048 | tf_op jit(solution)/shard_map/psum | solution.py:148
  306.3 6.3 %psum.30 = f32[2,128]{1,0:T(2,128)S(1)} all-reduce(f32[2,128]{1,0:T(2,128)S(1)} %bitcast.120), channel_id=1, replica_groups=mesh['section'=4,'seq'=8] {'section'}, use_global_device_ids=true, to_apply=%region_12.13 | all-reduce | flops 256 | bytes 2048 | tf_op jit(solution)/shard_map/psum | solution.py:154
  313.4 21.9 %psum.31 = f32[2]{0:T(128)} all-reduce(f32[2]{0:T(128)S(1)} %get-tuple-element.6), channel_id=1, replica_groups=mesh['section'=4,'seq'=8] {'seq'}, use_global_device_ids=true, to_apply=%region_14.15 | all-reduce | flops 2 | bytes 16 | tf_op jit(solution)/shard_map/psum | solution.py:162
  (86 shorter events, 22.2 us)
Async XLA Ops:
  7.2 55.5 %all-gather.6.cloned.1.call-start = ((), (), s32[]{:S(2)}) async-start(), calls=%async_computation.1 | async-start | bytes 1548288 | tf_op jit(solution)/shard_map/all_gather | solution.py:94
  7.9 90.5 %all-gather.8.cloned.1.call-start = ((), (), s32[]{:S(2)}) async-start(), calls=%async_computation.2 | async-start | bytes 1548288 | tf_op jit(solution)/shard_map/all_gather | solution.py:95
  8.6 169.8 %all-gather.10.cloned.1.call-start = ((), (), s32[]{:S(2)}) async-start(), calls=%async_computation.3 | async-start | bytes 3096576 | tf_op jit(solution)/shard_map/all_gather | solution.py:93
  9.4 235.9 %all-gather.12.cloned.1.call-start = ((), (), s32[]{:S(2)}) async-start(), calls=%async_computation.5 | async-start | bytes 3096576 | tf_op jit(solution)/shard_map/all_gather | solution.py:134
  10.0 281.9 %reduce-scatter.2.cloned.1.call-start = ((), (), s32[]{:S(2)}) async-start(), calls=%async_computation.4 | async-start | bytes 3440640 | tf_op jit(solution)/shard_map/reduce_scatter | solution.py:140
  58.4 39.9 %copy-start = (f32[256,2688]{0,1:T(8,128)}, f32[256,2688]{0,1:T(8,128)S(1)}, u32[]{:S(2)}) copy-start(f32[256,2688]{0,1:T(8,128)S(1)} %copy.55) | copy-start | bytes 8257540
  62.7 5.0 %copy-start.4 = (f32[128]{0:T(128)S(1)}, f32[128]{0:T(128)}, u32[]{:S(2)}) copy-start(f32[128]{0:T(128)} %param.21) | copy-start | bytes 1540
  100.9 10.1 %collective-permute-start = (bf16[2,128,512]{1,2,0:T(8,128)(2,1)S(1)}, bf16[2,128,512]{1,2,0:T(8,128)(2,1)S(1)}, u32[]{:S(2)}, u32[]{:S(2)}) collective-permute-start(bf16[2,128,512]{1,2,0:T(8,128)(2,1)S(1)} %pad_maximum_fusion), channel_id=1, source_target_pairs={} | collective-permute-start | bytes 786440 | tf_op jit(solution)/shard_map/ppermute | solution.py:17
  101.6 14.9 %collective-permute-start.1 = (bf16[2,128,512]{1,2,0:T(8,128)(2,1)S(1)}, bf16[2,128,512]{1,2,0:T(8,128)(2,1)S(1)}, u32[]{:S(2)}, u32[]{:S(2)}) collective-permute-start(bf16[2,128,512]{1,2,0:T(8,128)(2,1)S(1)} %pad_maximum_fusion), channel_id=1, source_target_pairs={{0,7},{8,15},{16,23},{24,31}} | collective-permute-start | bytes 786440 | tf_op jit(solution)/shard_map/ppermute | solution.py:17
  105.6 22.1 %collective-permute-start.2 = (bf16[2,128,512]{1,2,0:T(8,128)(2,1)S(1)}, bf16[2,128,512]{1,2,0:T(8,128)(2,1)S(1)}, u32[]{:S(2)}, u32[]{:S(2)}) collective-permute-start(bf16[2,128,512]{1,2,0:T(8,128)(2,1)S(1)} %pad_maximum_fusion), channel_id=1, source_target_pairs={{0,6},{1,7},{8,14},{9,15},{16,22},{17,23},{24,30},{25,31}} | collective-permute-start | bytes 786440 | tf_op jit(solution)/shard_map/ppermute | solution.py:17
  108.4 26.2 %collective-permute-start.3 = (bf16[2,128,512]{1,2,0:T(8,128)(2,1)S(1)}, bf16[2,128,512]{1,2,0:T(8,128)(2,1)S(1)}, u32[]{:S(2)}, u32[]{:S(2)}) collective-permute-start(bf16[2,128,512]{1,2,0:T(8,128)(2,1)S(1)} %pad_maximum_fusion), channel_id=1, source_target_pairs={{0,5},{1,6},{2,7},{8,13},{9,14},{10,15},{16,21},{17,22},{18,23},{2... | collective-permute-start | bytes 786440 | tf_op jit(solution)/shard_map/ppermute | solution.py:17
  109.7 30.5 %collective-permute-start.4 = (bf16[2,128,512]{1,2,0:T(8,128)(2,1)S(1)}, bf16[2,128,512]{1,2,0:T(8,128)(2,1)S(1)}, u32[]{:S(2)}, u32[]{:S(2)}) collective-permute-start(bf16[2,128,512]{1,2,0:T(8,128)(2,1)S(1)} %pad_maximum_fusion), channel_id=1, source_target_pairs={{0,4},{1,5},{2,6},{3,7},{8,12},{9,13},{10,14},{11,15},{16,20},{17,... | collective-permute-start | bytes 786440 | tf_op jit(solution)/shard_map/ppermute | solution.py:17
  111.1 34.8 %collective-permute-start.5 = (bf16[2,128,512]{1,2,0:T(8,128)(2,1)S(1)}, bf16[2,128,512]{1,2,0:T(8,128)(2,1)S(1)}, u32[]{:S(2)}, u32[]{:S(2)}) collective-permute-start(bf16[2,128,512]{1,2,0:T(8,128)(2,1)S(1)} %pad_maximum_fusion), channel_id=1, source_target_pairs={{0,3},{1,4},{2,5},{3,6},{4,7},{8,11},{9,12},{10,13},{11,14},{12,15... | collective-permute-start | bytes 786440 | tf_op jit(solution)/shard_map/ppermute | solution.py:17
  116.5 32.9 %collective-permute-start.6 = (bf16[2,128,512]{1,2,0:T(8,128)(2,1)S(1)}, bf16[2,128,512]{1,2,0:T(8,128)(2,1)S(1)}, u32[]{:S(2)}, u32[]{:S(2)}) collective-permute-start(bf16[2,128,512]{1,2,0:T(8,128)(2,1)S(1)} %pad_maximum_fusion), channel_id=1, source_target_pairs={{0,2},{1,3},{2,4},{3,5},{4,6},{5,7},{8,10},{9,11},{10,12},{11,13},... | collective-permute-start | bytes 786440 | tf_op jit(solution)/shard_map/ppermute | solution.py:17
  127.7 21.7 %collective-permute-start.7 = (bf16[2,128,512]{1,2,0:T(8,128)(2,1)S(1)}, bf16[2,128,512]{1,2,0:T(8,128)(2,1)S(1)}, u32[]{:S(2)}, u32[]{:S(2)}) collective-permute-start(bf16[2,128,512]{1,2,0:T(8,128)(2,1)S(1)} %pad_maximum_fusion), channel_id=1, source_target_pairs={{0,1},{1,2},{2,3},{3,4},{4,5},{5,6},{6,7},{8,9},{9,10},{10,11},{11... | collective-permute-start | bytes 786440 | tf_op jit(solution)/shard_map/ppermute | solution.py:17
  181.8 2.4 copy-start.5
  184.1 1.1 copy-start.1
  184.1 1.1 copy-start.3
  184.4 2.7 copy-start.2
  258.2 54.4 %copy-start.6 = (s32[2]{0:T(128)S(1)}, s32[2]{0:T(128)}, u32[]{:S(2)}) copy-start(s32[2]{0:T(128)} %param.15) | copy-start | bytes 28
  258.2 54.4 %copy-start.7 = (s32[2]{0:T(128)S(1)}, s32[2]{0:T(128)}, u32[]{:S(2)}) copy-start(s32[2]{0:T(128)} %param.14) | copy-start | bytes 28
Sparse Core Ops, SparseCore 0:
  10.2 45.0 all-gather.5
  57.4 40.9 all-gather.7
  100.6 77.8 all-gather.9
  180.4 64.8 all-gather.11
  258.3 33.5 reduce-scatter.1
